TPU v7x, 32 devices: a whole 2x2x4 slice. The times are simulated.
32 devices in a mesh: tok: 8 (over z, y), voc: 4 (over x, core).
Axes of the slice: x: 2, y: 2, z: 4, core: 2. Of those that a mesh axis runs over, the one named last changes fastest.
Arguments:
- teacher_logits: bfloat16 [1024, 76032], P('tok', 'voc'), may hold values from -1000 to 1000
- student_logits: bfloat16 [1024, 76032], P('tok', 'voc'), may hold values from -1000 to 1000
- target_ids: int32 [1024], P('tok'), may hold values from -1 to 76031, as said below
- vocab_used: int32 [76032], replicated, may hold values from 0 to 1
Outputs:
- logit_grad: bfloat16 [1024, 76032], P('tok', 'voc')
- token_loss: float32 [1024], P('tok')
Inputs may be any that keep to these rules, and one draw needn't show every extreme that they name: `target_ids`: every entry that is not -1 names a vocabulary entry v with vocab_used[v] == 1; the first token of every 128 is never -1.
All inputs are finite; a program needn't handle non-finite values.
Results may differ from a plain program's by a relative error of at most 0.0004.
Values may be sent and summed in bfloat16 or wider, within the bound.
No kernel may reach another device: no remote copies, remote signals or barrier semaphores. Data moves between devices by JAX's collectives and lax.ppermute only.
A program may use at most 64 MiB of HBM per device.

v0:
```python
import jax
import jax.numpy as jnp
from jax import lax
from jax.sharding import PartitionSpec as P

SENTINEL = -1e30


def combined_all(value, axis, join):
    pieces = jax.tree.map(lambda part: lax.all_gather(part, axis), value)
    head = jax.tree.map(lambda part: part[0], pieces)
    tail = jax.tree.map(lambda part: part[1:], pieces)
    subtotal, _ = lax.scan(lambda subtotal, slab: (join(subtotal, slab), None), head, tail)
    return subtotal


def local_totals(values, used):
    top_value = jnp.max(jnp.where(used, values, SENTINEL), axis=1)
    total = jnp.sum(jnp.where(used, jnp.exp(values - top_value[:, None]), 0.0), axis=1)
    return (top_value, total)


def merge_pair(first, second):
    top_value = jnp.maximum(first[0], second[0])
    total = first[1] * jnp.exp(first[0] - top_value) + second[1] * jnp.exp(second[0] - top_value)
    return (top_value, total)


def merge_joint(first, second):
    teacher_top = jnp.maximum(first[0], second[0])
    scale_one = jnp.exp(first[0] - teacher_top)
    scale_two = jnp.exp(second[0] - teacher_top)
    student_top, student_sum = merge_pair((first[3], first[4]), (second[3], second[4]))
    return (
        teacher_top,
        first[1] * scale_one + second[1] * scale_two,
        first[2] * scale_one + second[2] * scale_two,
        student_top,
        student_sum,
        first[5] + second[5],
    )


def body(teacher_logits, student_logits, target_ids, vocab_used):
    tok_rows, vocab_cols = teacher_logits.shape
    voc_count = lax.axis_size("voc")
    voc_index = lax.axis_index("voc")
    block_cols = vocab_cols // voc_count
    total_tokens = tok_rows * lax.axis_size("tok")
    kept = target_ids >= 0
    kept_count = lax.psum(jnp.sum(kept.astype(jnp.float32)), "tok")
    hard_weight = jnp.where(kept, 0.5 * total_tokens / kept_count, 0.0)
    position = jnp.arange(vocab_cols, dtype=jnp.int32)
    student_cols = (
        position // block_cols * voc_count + voc_index
    ) * block_cols + position % block_cols
    teacher_here = lax.all_to_all(
        teacher_logits.reshape(tok_rows, voc_count, block_cols),
        "voc",
        split_axis=1,
        concat_axis=1,
        tiled=True,
    ).reshape(tok_rows, vocab_cols)
    used = (vocab_used[student_cols] == 1)[None, :]
    onehot = student_cols[None, :] == target_ids[:, None]
    teacher = teacher_here.astype(jnp.float32)
    student = student_logits.astype(jnp.float32)
    student_top, student_sum = local_totals(student, used)
    target_part = jnp.sum(jnp.where(onehot, student, 0.0), axis=1)
    teacher_top, teacher_sum = local_totals(teacher, used)
    weighted = jnp.sum(
        jnp.where(used, jnp.exp(teacher - teacher_top[:, None]) * (teacher - student), 0.0), axis=1
    )
    teacher_top, teacher_sum, weighted, student_top, student_sum, target_logit = combined_all(
        (teacher_top, teacher_sum, weighted, student_top, student_sum, target_part),
        "voc",
        merge_joint,
    )
    teacher_lse = teacher_top + jnp.log(teacher_sum)
    student_lse = student_top + jnp.log(student_sum)
    teacher_prob = jnp.where(used, jnp.exp(teacher - teacher_lse[:, None]), 0.0)
    divergence = weighted / teacher_sum - teacher_lse + student_lse
    student_prob = jnp.where(used, jnp.exp(student - student_lse[:, None]), 0.0)
    gradient = 0.5 * (student_prob - teacher_prob) + hard_weight[:, None] * (
        student_prob - onehot.astype(jnp.float32)
    )
    gradient = jnp.where(used, gradient, 0.0).astype(jnp.bfloat16)
    token_loss = 0.5 * divergence + hard_weight * (student_lse - target_logit)
    return (gradient, token_loss)


def solution(mesh):
    placed = (P("tok", "voc"), P("tok", "voc"), P("tok"), P())
    return jax.shard_map(
        body, mesh=mesh, in_specs=placed, out_specs=(P("tok", "voc"), P("tok")), check_vma=False
    )
```

profile of v0, /device:TPU:0, one launch (start us, length us, event | category | flops | bytes accessed | tf_op | source)
XLA Modules:
  0.0 223.0 jit_solution(9439695803364014107)
XLA Ops:
  0.6 0.0 copy-start
  0.6 0.0 copy-start.1
  0.7 5.1 %all-to-all-start = ((bf16[128,4,4752]{0,2,1:T(8,128)(2,1)}), bf16[128,4,4752]{0,2,1:T(8,128)(2,1)}, u32[]{:S(2)}, u32[]{:S(2)}) async-start(bf16[128,4,4752]{0,2,1:T(8,128)(2,1)} %bitcast.95), calls=%async_computation | async-start | bytes 9732096 | tf_op jit(solution)/shard_map/all_to_all | solution.py:57
  5.8 0.0 copy-done.1
  5.8 0.6 fusion.55
  6.4 23.8 %psum.7 = f32[]{:T(128)} all-reduce(f32[]{:T(128)} %fusion.55), channel_id=1, replica_groups=mesh['tok'=8,'voc'=4] {'tok'}, use_global_device_ids=true, to_apply=%region_9.10 | all-reduce | flops 1 | bytes 8 | tf_op jit(solution)/shard_map/psum | solution.py:51
  30.1 0.6 fusion.51
  30.7 0.0 copy-done
  30.8 97.7 %gather_fusion = s32[19008]{0:T(1024)S(1)} fusion(s32[76032]{0:T(1024)S(1)} %copy-done, s32[19456]{0:T(1024)S(1)} %pad_clamp_fusion), kind=kCustom, calls=%fused_computation | custom fusion | bytes 228096 | tf_op jit(solution)/shard_map/gather | solution.py:64
  128.5 0.1 eq.28
  128.7 13.7 %fusion.27 = (f32[128]{0:T(128)S(1)}, f32[128]{0:T(128)S(1)}) fusion(bf16[128,19008]{0,1:T(8,128)(2,1)} %param.7, s32[128]{0:T(128)S(1)} %copy-done.1, s32[19008]{0:T(1024)S(1)} %fusion.48, pred[19008]{0:T(1024)(128)(4,1)S(1)} %broadcast_compare_fusion), kind=kLoop, calls=%fused_computation.42 | loop fusion | flops 14597888 | bytes 4962624 | tf_op jit(solution)/shard_map/reduce_sum | solution.py:69
  142.4 5.1 %all-gather.11 = f32[4,1,128]{2,1,0:T(1,128)S(1)} all-gather(f32[1,1,128]{2,1,0:T(1,128)S(1)} %bitcast.106), channel_id=7, replica_groups=mesh['tok'=8,'voc'=4] {'voc'}, dimensions={0}, use_global_device_ids=true | all-gather | bytes 2560 | tf_op jit(solution)/shard_map/all_gather | solution.py:10
  147.5 5.3 %all-gather.9 = f32[4,1,128]{2,1,0:T(1,128)S(1)} all-gather(f32[1,1,128]{2,1,0:T(1,128)S(1)} %bitcast.103), channel_id=5, replica_groups=mesh['tok'=8,'voc'=4] {'voc'}, dimensions={0}, use_global_device_ids=true | all-gather | bytes 2560 | tf_op jit(solution)/shard_map/all_gather | solution.py:10
  153.5 0.0 all-to-all-done
  153.5 10.4 %fusion.32 = f32[128]{0:T(128)S(1)} fusion(bf16[128,4,4752]{0,2,1:T(8,128)(2,1)} %all-to-all-done, pred[4,4752]{1,0:T(4,128)(4,1)S(1)} %eq.28), kind=kLoop, calls=%fused_computation.51 | loop fusion | flops 7298944 | bytes 4885568 | tf_op jit(solution)/shard_map/reduce_max | solution.py:18
  163.9 12.6 %fusion.26 = (f32[128]{0:T(128)S(1)}, f32[128]{0:T(128)S(1)}) fusion(bf16[128,19008]{0,1:T(8,128)(2,1)} %param.7, f32[128]{0:T(128)S(1)} %get-tuple-element.83, pred[19008]{0:T(1024)(128)(4,1)S(1)} %broadcast_compare_fusion, f32[128]{0:T(128)S(1)} %fusion.32, bf16[128,4,4752]{0,2,1:T(8,128)(2,1)} %all-to-all-done), kind=kLoop, calls=%fused_computation.41 | loop fusion | flops 24329984 | bytes 9753152 | tf_op jit(solution)/shard_map/reduce_sum | solution.py:19
  176.6 5.1 %all-gather.8 = f32[4,1,128]{2,1,0:T(1,128)S(1)} all-gather(f32[1,1,128]{2,1,0:T(1,128)S(1)} %bitcast.105), channel_id=4, replica_groups=mesh['tok'=8,'voc'=4] {'voc'}, dimensions={0}, use_global_device_ids=true | all-gather | bytes 2560 | tf_op jit(solution)/shard_map/all_gather | solution.py:10
  181.6 5.0 %all-gather.10 = f32[4,1,128]{2,1,0:T(1,128)S(1)} all-gather(f32[1,1,128]{2,1,0:T(1,128)S(1)} %bitcast.104), channel_id=6, replica_groups=mesh['tok'=8,'voc'=4] {'voc'}, dimensions={0}, use_global_device_ids=true | all-gather | bytes 2560 | tf_op jit(solution)/shard_map/all_gather | solution.py:10
  186.7 10.4 %fusion.35 = f32[128]{0:T(128)S(1)} fusion(bf16[128,4,4752]{0,2,1:T(8,128)(2,1)} %all-to-all-done, f32[128]{0:T(128)S(1)} %fusion.32, pred[4,4752]{1,0:T(4,128)(4,1)S(1)} %eq.28), kind=kLoop, calls=%fused_computation.54 | loop fusion | flops 9731968 | bytes 4886080 | tf_op jit(solution)/shard_map/reduce_sum | solution.py:19
  197.0 5.1 %all-gather.7 = f32[4,1,128]{2,1,0:T(1,128)S(1)} all-gather(f32[1,1,128]{2,1,0:T(1,128)S(1)} %bitcast.107), channel_id=3, replica_groups=mesh['tok'=8,'voc'=4] {'voc'}, dimensions={0}, use_global_device_ids=true | all-gather | bytes 2560 | tf_op jit(solution)/shard_map/all_gather | solution.py:10
  202.1 5.0 %all-gather.6 = f32[4,1,128]{2,1,0:T(1,128)S(1)} all-gather(f32[1,1,128]{2,1,0:T(1,128)S(1)} %bitcast.102), channel_id=2, replica_groups=mesh['tok'=8,'voc'=4] {'voc'}, dimensions={0}, use_global_device_ids=true | all-gather | bytes 2560 | tf_op jit(solution)/shard_map/all_gather | solution.py:10
  207.2 0.3 while.20
  207.5 0.5 multiply_add_fusion
  208.0 15.0 %fusion.19 = bf16[128,19008]{0,1:T(8,128)(2,1)} fusion(bf16[128,19008]{0,1:T(8,128)(2,1)} %param.7, bf16[128,4,4752]{0,2,1:T(8,128)(2,1)} %all-to-all-done, f32[128]{0:T(128)S(1)} %get-tuple-element.116, f32[128]{0:T(128)S(1)} %get-tuple-element.118, f32[128]{0:T(128)S(1)} %get-tuple-element.115, s32[128]{0:T(128)S(1)} %copy-done.1, s32[19008]{0:T(1024)S(1)} %fusion.48, ...), kind=kLoop, calls=%fused_computation.34 | loop fusion | flops 36495360 | bytes 14695232 | tf_op jit(solution)/shard_map/convert_element_type | solution.py:87
  (33 shorter events, 0.3 us)
Async XLA Ops:
  0.6 30.1 %copy-start = (s32[76032]{0:T(1024)S(1)}, s32[76032]{0:T(1024)}, u32[]{:S(2)}) copy-start(s32[76032]{0:T(1024)} %param.9) | copy-start | bytes 912388
  0.6 5.1 %copy-start.1 = (s32[128]{0:T(128)S(1)}, s32[128]{0:T(128)}, u32[]{:S(2)}) copy-start(s32[128]{0:T(128)} %param.8) | copy-start | bytes 1540
  0.7 152.9 %all-to-all-start = ((bf16[128,4,4752]{0,2,1:T(8,128)(2,1)}), bf16[128,4,4752]{0,2,1:T(8,128)(2,1)}, u32[]{:S(2)}, u32[]{:S(2)}) async-start(bf16[128,4,4752]{0,2,1:T(8,128)(2,1)} %bitcast.95), calls=%async_computation | async-start | bytes 9732096 | tf_op jit(solution)/shard_map/all_to_all | solution.py:57
where the time goes:
time: 224 us; the launch traced here: 223 us
  local copies, waits for them, and re-layouts  97.9 us (44%)
  other arithmetic  64.1 us (29%)
  blocking collectives  54.4 us (24%)
  starting transfers between devices  5.11 us (2%)
    gather x1, local copies, waits for them, and re-layouts, body(): used = (vocab_used[student_cols] == 1)[None, :]  97.7 us
    all_gather x6, blocking collectives, combined_all(): pieces = jax.tree.map(lambda part: lax.all_gather(part, axis), value)  30.6 us
    psum x1, blocking collectives, body(): kept_count = lax.psum(jnp.sum(kept.astype(jnp.float32)), 'tok')  23.8 us
    reduce_sum x2, other arithmetic, local_totals(): jnp.sum(jnp.where(used, jnp.exp(values - top_value[:, None]), 0.0), axis=1)  23 us
    convert_element_type x1, other arithmetic, body(): gradient = jnp.where(used, gradient, 0.0).astype(jnp.bfloat16)  15 us
    reduce_sum x1, other arithmetic, body(): target_part = jnp.sum(jnp.where(onehot, student, 0.0), axis=1)  13.7 us
    reduce_max x1, other arithmetic, local_totals(): top_value = jnp.max(jnp.where(used, values, SENTINEL), axis=1)  10.4 us
    all_to_all x1, starting transfers between devices, body(): lax.all_to_all(teacher_logits.reshape(tok_rows, voc_count, block_cols), '...  5.11 us
  transfers between devices with their start and end apart: 1, of which 0 were waited for; matrix products, arithmetic and copies ran while one was open for 51% of the time, Pallas kernels for 0%

commit v1 on v0

--- a/solution.py
+++ b/solution.py
@@ -54,12 +54,20 @@
     student_cols = (
         position // block_cols * voc_count + voc_index
     ) * block_cols + position % block_cols
-    teacher_here = lax.all_to_all(
-        teacher_logits.reshape(tok_rows, voc_count, block_cols),
-        "voc",
-        split_axis=1,
-        concat_axis=1,
-        tiled=True,
+    teacher_here = jnp.concatenate(
+        lax.all_to_all(
+            jnp.stack(
+                jnp.split(
+                    teacher_logits.reshape(tok_rows, voc_count, block_cols),
+                    lax.axis_size("voc"),
+                    axis=1,
+                )
+            ),
+            "voc",
+            0,
+            0,
+        ),
+        axis=1,
     ).reshape(tok_rows, vocab_cols)
     used = (vocab_used[student_cols] == 1)[None, :]
     onehot = student_cols[None, :] == target_ids[:, None]

time: 224 us -> 230 us (1.027)
  local copies, waits for them, and re-layouts: 97.9 us -> 101 us
  other arithmetic: 64.1 us -> 67 us
    another operation x0 -> x1, other arithmetic: none -> 2.74 us  [body(): jnp.stack(jnp.split(teacher_logits.reshape(tok_rows, voc_count, block_col...]
    another operation x0 -> x1, local copies, waits for them, and re-layouts: none -> 2.74 us  [body(): jnp.stack(jnp.split(teacher_logits.reshape(tok_rows, voc_count, block_col...]
  transfers between devices with their start and end apart: 1 -> 1, of which waited for: 0 -> 0; matrix products, arithmetic and copies ran while one was open for 51% -> 49% of each run, Pallas kernels for 0% -> 0%
where the time goes in v1:
time: 230 us; the launch traced here: 229 us
  local copies, waits for them, and re-layouts  101 us (44%)
  other arithmetic  67 us (29%)
  blocking collectives  54.4 us (24%)
  starting transfers between devices  5.1 us (2%)
    gather x1, local copies, waits for them, and re-layouts, body(): used = (vocab_used[student_cols] == 1)[None, :]  97.7 us
    all_gather x6, blocking collectives, combined_all(): pieces = jax.tree.map(lambda part: lax.all_gather(part, axis), value)  30.6 us
    psum x1, blocking collectives, body(): kept_count = lax.psum(jnp.sum(kept.astype(jnp.float32)), 'tok')  23.8 us
    reduce_sum x2, other arithmetic, local_totals(): jnp.sum(jnp.where(used, jnp.exp(values - top_value[:, None]), 0.0), axis=1)  23 us
    convert_element_type x1, other arithmetic, body(): gradient = jnp.where(used, gradient, 0.0).astype(jnp.bfloat16)  15.1 us
    reduce_sum x1, other arithmetic, body(): target_part = jnp.sum(jnp.where(onehot, student, 0.0), axis=1)  13.7 us
    reduce_max x1, other arithmetic, local_totals(): top_value = jnp.max(jnp.where(used, values, SENTINEL), axis=1)  10.4 us
    all_to_all x1, starting transfers between devices, body(): lax.all_to_all(jnp.stack(jnp.split(teacher_logits.reshape(tok_rows, voc_c...  5.1 us
  transfers between devices with their start and end apart: 1, of which 0 were waited for; matrix products, arithmetic and copies ran while one was open for 49% of the time, Pallas kernels for 0%

profile of v1, /device:TPU:0, one launch (start us, length us, event | category | flops | bytes accessed | tf_op | source)
XLA Modules:
  0.0 228.7 jit_solution(3239623152381461153)
XLA Ops:
  0.6 0.0 copy-start
  0.6 2.7 %slice_bitcast_fusion.3 = (bf16[1,128,1,4752]{1,3,2,0:T(8,128)(2,1)S(1)}, bf16[1,128,1,4752]{1,3,2,0:T(8,128)(2,1)S(1)}, bf16[1,128,1,4752]{1,3,2,0:T(8,128)(2,1)S(1)}, bf16[1,128,1,4752]{1,3,2,0:T(8,128)(2,1)S(1)}) fusion(bf16[128,4,4752]{0,2,1:T(8,128)(2,1)} %bitcast.105), kind=kLoop, calls=%fused_computation.62 | loop fusion | bytes 9732096 | tf_op jit(solution)/shard_map/stack | solution.py:59
  3.4 2.7 %pad_maximum_fusion = bf16[4,128,1,4752]{1,3,2,0:T(8,128)(2,1)} fusion(bf16[1,128,1,4752]{1,3,2,0:T(8,128)(2,1)S(1)} %get-tuple-element.119, bf16[1,128,1,4752]{1,3,2,0:T(8,128)(2,1)S(1)} %get-tuple-element.120, bf16[1,128,1,4752]{1,3,2,0:T(8,128)(2,1)S(1)} %get-tuple-element.121, bf16[1,128,1,4752]{1,3,2,0:T(8,128)(2,1)S(1)} %get-tuple-element.118), kind=kLoop, calls=%fused_computation.58 | loop fusion | flops 7299072 | bytes 9732096 | tf_op jit(solution)/shard_map/stack | solution.py:59
  6.1 0.0 copy-start.1
  6.1 5.1 %all-to-all-start = ((bf16[4,128,1,4752]{1,3,2,0:T(8,128)(2,1)}), bf16[4,128,1,4752]{1,3,2,0:T(8,128)(2,1)}, u32[]{:S(2)}, u32[]{:S(2)}) async-start(bf16[4,128,1,4752]{1,3,2,0:T(8,128)(2,1)} %pad_maximum_fusion), calls=%async_computation | async-start | bytes 9732096 | tf_op jit(solution)/shard_map/all_to_all | solution.py:58
  11.2 0.0 copy-done.1
  11.3 0.6 fusion.55
  11.9 23.8 %psum.7 = f32[]{:T(128)} all-reduce(f32[]{:T(128)} %fusion.55), channel_id=1, replica_groups=mesh['tok'=8,'voc'=4] {'tok'}, use_global_device_ids=true, to_apply=%region_9.10 | all-reduce | flops 1 | bytes 8 | tf_op jit(solution)/shard_map/psum | solution.py:51
  35.7 0.6 fusion.51
  36.3 0.0 copy-done
  36.3 97.7 %gather_fusion = s32[19008]{0:T(1024)S(1)} fusion(s32[76032]{0:T(1024)S(1)} %copy-done, s32[19456]{0:T(1024)S(1)} %pad_clamp_fusion), kind=kCustom, calls=%fused_computation | custom fusion | bytes 228096 | tf_op jit(solution)/shard_map/gather | solution.py:72
  134.1 0.1 eq.28
  134.2 13.7 %fusion.27 = (f32[128]{0:T(128)S(1)}, f32[128]{0:T(128)S(1)}) fusion(bf16[128,19008]{0,1:T(8,128)(2,1)} %param.7, s32[128]{0:T(128)S(1)} %copy-done.1, s32[19008]{0:T(1024)S(1)} %fusion.48, pred[19008]{0:T(1024)(128)(4,1)S(1)} %broadcast_compare_fusion), kind=kLoop, calls=%fused_computation.42 | loop fusion | flops 14597888 | bytes 4962624 | tf_op jit(solution)/shard_map/reduce_sum | solution.py:77
  148.0 5.1 %all-gather.9 = f32[4,1,128]{2,1,0:T(1,128)S(1)} all-gather(f32[1,1,128]{2,1,0:T(1,128)S(1)} %bitcast.113), channel_id=5, replica_groups=mesh['tok'=8,'voc'=4] {'voc'}, dimensions={0}, use_global_device_ids=true | all-gather | bytes 2560 | tf_op jit(solution)/shard_map/all_gather | solution.py:10
  153.0 5.3 %all-gather.11 = f32[4,1,128]{2,1,0:T(1,128)S(1)} all-gather(f32[1,1,128]{2,1,0:T(1,128)S(1)} %bitcast.115), channel_id=7, replica_groups=mesh['tok'=8,'voc'=4] {'voc'}, dimensions={0}, use_global_device_ids=true | all-gather | bytes 2560 | tf_op jit(solution)/shard_map/all_gather | solution.py:10
  159.1 0.0 all-to-all-done
  159.1 10.4 %fusion.32 = f32[128]{0:T(128)S(1)} fusion(bf16[4,128,1,4752]{1,3,2,0:T(8,128)(2,1)} %all-to-all-done, pred[4,4752]{1,0:T(4,128)(4,1)S(1)} %eq.28), kind=kLoop, calls=%fused_computation.51 | loop fusion | flops 7298944 | bytes 4885568 | tf_op jit(solution)/shard_map/reduce_max | solution.py:18
  169.5 12.6 %fusion.26 = (f32[128]{0:T(128)S(1)}, f32[128]{0:T(128)S(1)}) fusion(bf16[128,19008]{0,1:T(8,128)(2,1)} %param.7, f32[128]{0:T(128)S(1)} %get-tuple-element.83, pred[19008]{0:T(1024)(128)(4,1)S(1)} %broadcast_compare_fusion, f32[128]{0:T(128)S(1)} %fusion.32, bf16[4,128,1,4752]{1,3,2,0:T(8,128)(2,1)} %all-to-all-done), kind=kLoop, calls=%fused_computation.41 | loop fusion | flops 24329984 | bytes 9753152 | tf_op jit(solution)/shard_map/reduce_sum | solution.py:19
  182.1 5.1 %all-gather.10 = f32[4,1,128]{2,1,0:T(1,128)S(1)} all-gather(f32[1,1,128]{2,1,0:T(1,128)S(1)} %bitcast.116), channel_id=6, replica_groups=mesh['tok'=8,'voc'=4] {'voc'}, dimensions={0}, use_global_device_ids=true | all-gather | bytes 2560 | tf_op jit(solution)/shard_map/all_gather | solution.py:10
  187.2 5.0 %all-gather.8 = f32[4,1,128]{2,1,0:T(1,128)S(1)} all-gather(f32[1,1,128]{2,1,0:T(1,128)S(1)} %bitcast.114), channel_id=4, replica_groups=mesh['tok'=8,'voc'=4] {'voc'}, dimensions={0}, use_global_device_ids=true | all-gather | bytes 2560 | tf_op jit(solution)/shard_map/all_gather | solution.py:10
  192.3 10.4 %fusion.35 = f32[128]{0:T(128)S(1)} fusion(bf16[4,128,1,4752]{1,3,2,0:T(8,128)(2,1)} %all-to-all-done, f32[128]{0:T(128)S(1)} %fusion.32, pred[4,4752]{1,0:T(4,128)(4,1)S(1)} %eq.28), kind=kLoop, calls=%fused_computation.54 | loop fusion | flops 9731968 | bytes 4886080 | tf_op jit(solution)/shard_map/reduce_sum | solution.py:19
  202.6 5.1 %all-gather.7 = f32[4,1,128]{2,1,0:T(1,128)S(1)} all-gather(f32[1,1,128]{2,1,0:T(1,128)S(1)} %bitcast.117), channel_id=3, replica_groups=mesh['tok'=8,'voc'=4] {'voc'}, dimensions={0}, use_global_device_ids=true | all-gather | bytes 2560 | tf_op jit(solution)/shard_map/all_gather | solution.py:10
  207.7 5.0 %all-gather.6 = f32[4,1,128]{2,1,0:T(1,128)S(1)} all-gather(f32[1,1,128]{2,1,0:T(1,128)S(1)} %bitcast.112), channel_id=2, replica_groups=mesh['tok'=8,'voc'=4] {'voc'}, dimensions={0}, use_global_device_ids=true | all-gather | bytes 2560 | tf_op jit(solution)/shard_map/all_gather | solution.py:10
  212.8 0.3 while.20
  213.1 0.5 multiply_add_fusion
  213.6 15.1 %fusion.19 = bf16[128,19008]{0,1:T(8,128)(2,1)} fusion(bf16[128,19008]{0,1:T(8,128)(2,1)} %param.7, bf16[4,128,1,4752]{1,3,2,0:T(8,128)(2,1)} %all-to-all-done, f32[128]{0:T(128)S(1)} %get-tuple-element.116, f32[128]{0:T(128)S(1)} %get-tuple-element.122, f32[128]{0:T(128)S(1)} %get-tuple-element.115, s32[128]{0:T(128)S(1)} %copy-done.1, ...), kind=kLoop, calls=%fused_computation.34 | loop fusion | flops 36495360 | bytes 14695232 | tf_op jit(solution)/shard_map/convert_element_type | solution.py:95
  (33 shorter events, 0.3 us)
Async XLA Ops:
  0.6 35.7 %copy-start = (s32[76032]{0:T(1024)S(1)}, s32[76032]{0:T(1024)}, u32[]{:S(2)}) copy-start(s32[76032]{0:T(1024)} %param.9) | copy-start | bytes 912388
  6.1 5.1 %copy-start.1 = (s32[128]{0:T(128)S(1)}, s32[128]{0:T(128)}, u32[]{:S(2)}) copy-start(s32[128]{0:T(128)} %param.8) | copy-start | bytes 1540
  6.1 153.0 %all-to-all-start = ((bf16[4,128,1,4752]{1,3,2,0:T(8,128)(2,1)}), bf16[4,128,1,4752]{1,3,2,0:T(8,128)(2,1)}, u32[]{:S(2)}, u32[]{:S(2)}) async-start(bf16[4,128,1,4752]{1,3,2,0:T(8,128)(2,1)} %pad_maximum_fusion), calls=%async_computation | async-start | bytes 9732096 | tf_op jit(solution)/shard_map/all_to_all | solution.py:58
